TPU v7x, 32 devices: a whole 2x2x4 slice. The times are simulated.
32 devices in a mesh: plane: 2 (over x), coil: 16 (over z, y, core).
Axes of the slice: x: 2, y: 2, z: 4, core: 2. Of those that a mesh axis runs over, the one named last changes fastest.
Arguments:
- image: float32 [512, 8, 512], P(('plane', 'coil')), parts along dimension 0, may hold values from -6 to 6
- sens: float32 [512, 32, 512], P(('plane', 'coil')), parts along dimension 0, may hold values from -0.75 to 0.75
- kspace: float32 [512, 256, 512], P('plane', 'coil'), parts along dimension 0, may hold values from -6 to 6
- mask: int32 [8, 256], replicated, may hold values 0 or 1
Outputs:
- recon: float32 [512, 8, 512], P(('plane', 'coil')), parts along dimension 0
There are 2 independent parts, one for each index of `plane`. A program takes and returns all parts, laid end to end along the dimension named above; an argument that names none is the same for every part. Nothing has to cross between parts.
Inputs may be any that keep to these rules, and one draw needn't show every extreme that they name: mask[f, ky] is 1 where phase-encode line ky is sampled in frame f, else 0.
All inputs are finite; a program needn't handle non-finite values.
Results may differ from a plain program's by a relative error of at most 0.0001.
Values sent between devices are 32-bit elements; how exact they have to be, the bound alone decides.
A program may use at most 128 MiB of HBM per device.

v0:
```python
import jax
import jax.numpy as jnp
from jax import lax
from jax.sharding import PartitionSpec as P

OUTER = 2
INNER = 2


step_size = 0.5
tv_weight = 0.1
dual_step = 1.25
highest = lax.Precision.HIGHEST


def shifted(block, axis, distance):
    devices = range(lax.axis_size(axis))
    route = [(i - distance, i) for i in devices if i - distance in devices]
    return lax.ppermute(block, axis, route)


def dft_tables(length):
    index = lax.iota(jnp.int32, length)
    product = index[:, None] * index[None, :] % length
    angle = 2.0 * jnp.pi / length * product.astype(jnp.float32)
    scale = 1.0 / jnp.sqrt(jnp.float32(length))
    return (jnp.cos(angle) * scale, -jnp.sin(angle) * scale)


def column_matrix(cos_part, sin_part):
    upper = jnp.concatenate([cos_part, sin_part], 1)
    lower = jnp.concatenate([-sin_part, cos_part], 1)
    return jnp.concatenate([upper, lower], 0)


def swap_parts(field):
    half = field.shape[-1] // 2
    return jnp.concatenate([-field[..., half:], field[..., :half]], -1)


def mul_packed(left, right):
    half = left.shape[-1] // 2
    left_re, left_im = (left[..., :half], left[..., half:])
    right_re, right_im = (right[..., :half], right[..., half:])
    return jnp.concatenate(
        [left_re * right_re - left_im * right_im, left_re * right_im + left_im * right_re], -1
    )


def mul_conj(left, right):
    half = left.shape[-1] // 2
    left_re, left_im = (left[..., :half], left[..., half:])
    right_re, right_im = (right[..., :half], right[..., half:])
    return jnp.concatenate(
        [left_re * right_re + left_im * right_im, left_re * right_im - left_im * right_re], -1
    )


def rows_apply(cos_part, sin_part, field):
    first = jnp.einsum(
        "ky,ypz->kpz", cos_part, field, precision=highest, preferred_element_type=jnp.float32
    )
    second = jnp.einsum(
        "ky,ypz->kpz",
        sin_part,
        swap_parts(field),
        precision=highest,
        preferred_element_type=jnp.float32,
    )
    return first + second


def cols_apply(matrix, field):
    shape_in = field.shape
    flat = field.reshape(-1, shape_in[-1])
    return jnp.dot(flat, matrix, precision=highest, preferred_element_type=jnp.float32).reshape(
        shape_in
    )


def pair_rows(proj_re, proj_im, field):
    first = jnp.einsum(
        "pay,ypz->apz", proj_re, field, precision=highest, preferred_element_type=jnp.float32
    )
    second = jnp.einsum(
        "pay,ypz->apz",
        proj_im,
        swap_parts(field),
        precision=highest,
        preferred_element_type=jnp.float32,
    )
    return first + second


def forward_diff(field, keep_rows):
    after = shifted(field[:1], "coil", -1)
    following = jnp.concatenate([field[1:], after], 0)
    diff_rows = jnp.where(keep_rows, following - field, 0.0)
    diff_time = jnp.concatenate([field[:, 1:] - field[:, :-1], jnp.zeros_like(field[:, :1])], 1)
    return (diff_time, diff_rows)


def adjoint_diff(dual_time, dual_rows, keep_rows):
    before = shifted(dual_rows[-1:], "coil", 1)
    keep_time = (lax.iota(jnp.int32, dual_time.shape[1]) < dual_time.shape[1] - 1)[None, :, None]
    from_time = jnp.concatenate(
        [jnp.zeros_like(dual_time[:, :1]), dual_time[:, :-1]], 1
    ) - jnp.where(keep_time, dual_time, 0.0)
    from_rows = jnp.concatenate([before, dual_rows[:-1]], 0) - jnp.where(keep_rows, dual_rows, 0.0)
    return from_time + from_rows


def per_device(image, sens, kspace, mask):
    rows_dev, frame_count, packed = image.shape
    coil_count = sens.shape[1]
    length, pair_count, unused = kspace.shape
    half = packed // 2
    device = lax.axis_index("coil")
    global_rows = device * rows_dev + lax.iota(jnp.int32, rows_dev)
    keep_rows = (global_rows < length - 1)[:, None, None]
    frame_ids = (device * pair_count + lax.iota(jnp.int32, pair_count)) % frame_count
    onehot = (frame_ids[:, None] == lax.iota(jnp.int32, frame_count)[None, :]).astype(jnp.float32)
    mask_pairs = jnp.dot(
        onehot, mask.astype(jnp.float32), precision=highest, preferred_element_type=jnp.float32
    )
    mask_rows = jnp.transpose(mask_pairs)
    sampled = mask_rows[:, :, None]
    row_cos, row_sin = dft_tables(length)
    col_cos, col_sin = dft_tables(half)
    adjoint_cols = column_matrix(col_cos, -col_sin)
    repeated = jnp.broadcast_to(sens[:, :, None, :], (rows_dev, coil_count, frame_count, packed))
    maps_pairs = lax.all_to_all(
        repeated.reshape(rows_dev, coil_count * frame_count, packed),
        "coil",
        split_axis=1,
        concat_axis=0,
        tiled=True,
    )
    proj_re = jnp.einsum(
        "ka,kp,ky->pay",
        row_cos,
        mask_rows,
        row_cos,
        precision=highest,
        preferred_element_type=jnp.float32,
    )
    proj_re = proj_re + jnp.einsum(
        "ka,kp,ky->pay",
        row_sin,
        mask_rows,
        row_sin,
        precision=highest,
        preferred_element_type=jnp.float32,
    )
    proj_im = jnp.einsum(
        "ka,kp,ky->pay",
        row_cos,
        mask_rows,
        row_sin,
        precision=highest,
        preferred_element_type=jnp.float32,
    )
    proj_im = proj_im - jnp.einsum(
        "ka,kp,ky->pay",
        row_sin,
        mask_rows,
        row_cos,
        precision=highest,
        preferred_element_type=jnp.float32,
    )
    base = cols_apply(adjoint_cols, rows_apply(row_cos, -row_sin, sampled * kspace))
    field = image
    for sweep in range(OUTER):
        chosen = jnp.einsum(
            "rfz,pf->rpz",
            lax.all_gather(field, "coil", axis=0, tiled=True),
            onehot,
            precision=highest,
            preferred_element_type=jnp.float32,
        )
        coil_images = mul_packed(maps_pairs, chosen)
        coil_grads = pair_rows(proj_re, proj_im, coil_images) - base
        weighted = mul_conj(maps_pairs, coil_grads)
        gradient = lax.psum_scatter(
            jnp.einsum(
                "rpz,pf->rfz",
                weighted,
                onehot,
                precision=highest,
                preferred_element_type=jnp.float32,
            ),
            "coil",
            scatter_dimension=0,
            tiled=True,
        )
        target = field - step_size * gradient
        dual_time = jnp.zeros_like(target)
        dual_rows = jnp.zeros_like(target)
        for repeat in range(INNER):
            if repeat == 0:
                primal = target
            else:
                primal = target - tv_weight * adjoint_diff(dual_time, dual_rows, keep_rows)
            diff_time, diff_rows = forward_diff(primal, keep_rows)
            dual_time = jnp.clip(dual_time + dual_step * diff_time, -1.0, 1.0)
            dual_rows = jnp.clip(dual_rows + dual_step * diff_rows, -1.0, 1.0)
        field = target - tv_weight * adjoint_diff(dual_time, dual_rows, keep_rows)
    return field


def solution(mesh):
    return jax.shard_map(
        per_device,
        mesh=mesh,
        in_specs=(
            P(("plane", "coil"), None, None),
            P(("plane", "coil"), None, None),
            P("plane", "coil", None),
            P(),
        ),
        out_specs=P(("plane", "coil"), None, None),
        check_vma=False,
    )
```

profile of v0, /device:TPU:0, one launch (start us, length us, event | category | flops | bytes accessed | tf_op | source)
XLA Modules:
  0.0 705.2 jit_solution(16049533103693490658)
XLA Ops:
  6.5 1.8 copy.32
  8.4 4.4 broadcast_in_dim.86
  12.7 7.6 %all-to-all-start = ((f32[16,256,512]{2,0,1:T(8,128)}), f32[16,256,512]{2,0,1:T(8,128)}, u32[]{:S(2)}, u32[]{:S(2)}) async-start(f32[16,256,512]{2,0,1:T(8,128)} %bitcast.60), calls=%async_computation | async-start | bytes 16777216 | tf_op jit(solution)/shard_map/all_to_all | solution.py:132
  23.6 4.6 fusion.22
  28.2 4.6 fusion.24
  32.8 7.5 %fusion.42 = f32[16,256,256]{2,1,0:T(8,128)} fusion(f32[16,256,256]{2,1,0:T(8,128)S(1)} %fusion.22, f32[256,256]{0,1:T(8,128)S(1)} %copy.35, f32[256,16]{0,1:T(8,128)S(1)} %convolution_bitcast_fusion.2), kind=kOutput, calls=%fused_computation.52 | convolution fusion | flops 3224371200 | bytes 8667136 | tf_op jit(solution)/shard_map/ka,kp,ky->pay/dot_general | solution.py:155
  40.4 7.1 %fusion.39 = f32[16,256,256]{2,1,0:T(8,128)} fusion(f32[16,256,256]{2,1,0:T(8,128)S(1)} %fusion.24, f32[256,256]{0,1:T(8,128)S(1)} %copy.35, f32[256,16]{0,1:T(8,128)S(1)} %convolution_bitcast_fusion.2), kind=kOutput, calls=%fused_computation.51 | convolution fusion | flops 3224305664 | bytes 8667136 | tf_op jit(solution)/shard_map/ka,kp,ky->pay/dot_general | solution.py:139
  47.5 4.9 copy_multiply_fusion
  52.4 2.7 slice_negate_fusion
  55.0 9.7 %fusion.91 = f32[256,16,512]{2,0,1:T(8,128)S(1)} fusion(f32[256,16,512]{2,0,1:T(8,128)S(1)} %copy_multiply_fusion), kind=kOutput, calls=%fused_computation.116 | convolution fusion | flops 6443433984 | bytes 16777216 | tf_op jit(solution)/shard_map/ky,ypz->kpz/dot_general | solution.py:60
  64.7 12.3 %fusion.30 = f32[256,16,512]{2,0,1:T(8,128)} fusion(f32[256,16,512]{2,0,1:T(8,128)S(1)} %fusion.91, f32[256,16,256]{2,0,1:T(8,128)} %get-tuple-element.16, f32[256,16,256]{2,0,1:T(8,128)S(1)} %get-tuple-element.15), kind=kOutput, calls=%fused_computation.46 | convolution fusion | flops 6447759360 | bytes 25165824 | tf_op jit(solution)/shard_map/ky,ypz->kpz/dot_general | solution.py:63
  77.0 95.4 %all-gather.3.cloned.1.call-done = f32[256,8,512]{2,1,0:T(8,128)} async-done(((f32[16,8,512]{2,1,0:T(8,128)}), f32[256,8,512]{2,1,0:T(8,128)}) %all-gather.3.cloned.1.call-update) | async-done | bytes 4194320 | tf_op jit(solution)/shard_map/all_gather | solution.py:176
  172.4 7.6 %convolution_bitcast_fusion.1 = f32[256,16,512]{2,1,0:T(8,128)} fusion(f32[256,8,512]{2,1,0:T(8,128)} %all-gather.3.cloned.1.call-done, s32[16]{0:T(128)S(1)} %and_select_fusion), kind=kOutput, calls=%fused_computation.48 | convolution fusion | flops 201326720 | bytes 12582976 | tf_op jit(solution)/shard_map/rfz,pf->rpz/dot_general | solution.py:174
  180.0 16.2 %all-to-all-done = f32[16,256,512]{2,0,1:T(8,128)} async-done(((f32[16,256,512]{2,0,1:T(8,128)}), f32[16,256,512]{2,0,1:T(8,128)}, u32[]{:S(2)}, u32[]{:S(2)}) %all-to-all-start) | async-done | bytes 8388640 | tf_op jit(solution)/shard_map/all_to_all | solution.py:132
  196.2 10.1 %copy.34 = f32[16,16,16,512]{3,2,1,0:T(8,128)S(1)} copy(f32[16,16,16,512]{3,1,2,0:T(8,128)} %bitcast.4) | data formatting | bytes 16777216 | tf_op jit(solution)/shard_map/all_to_all | solution.py:132
  206.3 6.9 fusion.148
  213.4 10.3 %pad_maximum_fusion.1 = (f32[256,16,512]{2,1,0:T(8,128)S(1)}, f32[256,16,512]{2,1,0:T(8,128)}) fusion(f32[256,16,256]{2,1,0:T(8,128)} %get-tuple-element.14, f32[256,16,256]{2,1,0:T(8,128)} %get-tuple-element.7, f32[256,16,256]{2,1,0:T(8,128)} %get-tuple-element.8), kind=kLoop, calls=%fused_computation.1 | loop fusion | flops 4194304 | bytes 29360128 | tf_op jit(solution)/shard_map/concatenate | solution.py:38
  223.7 18.6 %fusion.18 = f32[16,512,256]{2,1,0:T(8,128)} fusion(f32[16,256,256]{2,1,0:T(8,128)S(1)} %copy-done.1, f32[256,16,512]{2,1,0:T(8,128)S(1)} %get-tuple-element.19), kind=kOutput, calls=%fused_computation.25 | convolution fusion | flops 6442450944 | bytes 20971520 | tf_op jit(solution)/shard_map/pay,ypz->apz/dot_general | solution.py:85
  242.3 10.5 %copy.40 = f32[16,512,256]{1,0,2:T(8,128)} copy(f32[16,512,256]{2,1,0:T(8,128)} %fusion.18) | data formatting | bytes 16777216 | tf_op jit(solution)/shard_map/pay,ypz->apz/dot_general | solution.py:85
  252.8 23.8 %fusion.20 = f32[16,512,256]{2,1,0:T(8,128)} fusion(f32[16,256,256]{2,1,0:T(8,128)} %fusion.39, f32[256,16,512]{2,1,0:T(8,128)} %get-tuple-element.20), kind=kOutput, calls=%fused_computation.27 | convolution fusion | flops 6442450944 | bytes 20971520 | tf_op jit(solution)/shard_map/pay,ypz->apz/dot_general | solution.py:82
  276.6 10.5 %copy.39 = f32[16,512,256]{1,0,2:T(8,128)} copy(f32[16,512,256]{2,1,0:T(8,128)} %fusion.20) | data formatting | bytes 16777216 | tf_op jit(solution)/shard_map/pay,ypz->apz/dot_general | solution.py:82
  287.0 27.0 %bitcast_subtract_fusion.1 = (f32[256,16,512]{2,1,0:T(8,128)}, f32[256,16,512]{2,1,0:T(8,128)}) fusion(f32[16,512,256]{1,0,2:T(8,128)} %copy.39, f32[16,512,256]{1,0,2:T(8,128)} %copy.40, f32[256,256]{1,0:T(8,128)S(1)} %get-tuple-element.24, f32[256,256]{1,0:T(8,128)S(1)} %get-tuple-element.23, f32[256,256]{1,0:T(8,128)S(1)} %fusion.98, ...), kind=kOutput, calls=%fused_computation.17 | convolution fusion | flops 12889882624 | bytes 42729472 | tf_op jit(solution)/shard_map/dot_general | solution.py:76
  314.0 6.9 multiply_add_fusion.2
  320.9 5.7 fusion.36
  326.7 104.7 %reduce-scatter.3.cloned.1.call-done = f32[16,8,512]{2,1,0:T(8,128)} async-done(((f32[256,8,512]{2,1,0:T(8,128)}), f32[16,8,512]{2,1,0:T(8,128)}) %reduce-scatter.3.cloned.1.call-update) | async-done | bytes 262160 | tf_op jit(solution)/shard_map/reduce_scatter | solution.py:184
  432.4 1.3 collective-permute-start
  433.8 1.7 collective-permute-done
  435.6 2.7 collective-permute-start.1
  439.3 1.3 collective-permute-start.2
  440.6 1.7 collective-permute-done.2
  442.5 4.5 collective-permute-start.3
  448.7 52.8 %all-gather.5.cloned.1.call-done = f32[256,8,512]{2,1,0:T(8,128)} async-done(((f32[16,8,512]{2,1,0:T(8,128)}), f32[256,8,512]{2,1,0:T(8,128)}) %all-gather.5.cloned.1.call-update) | async-done | bytes 4194320 | tf_op jit(solution)/shard_map/all_gather | solution.py:176
  501.5 6.7 convolution_bitcast_fusion
  508.3 8.2 %fusion.147 = (f32[256,16,256]{2,1,0:T(8,128)}, f32[256,16,256]{2,1,0:T(8,128)}, f32[256,16,256]{2,1,0:T(8,128)}) fusion(f32[256,16,512]{2,1,0:T(8,128)S(1)} %convolution_bitcast_fusion, f32[256,16,512]{2,1,0:T(8,128)} %bitcast.58), kind=kLoop, calls=%fused_computation.181 | loop fusion | flops 7340032 | bytes 29360128 | tf_op jit(solution)/shard_map/neg | solution.py:38
  516.5 10.2 %pad_maximum_fusion.3 = (f32[256,16,512]{2,1,0:T(8,128)S(1)}, f32[256,16,512]{2,1,0:T(8,128)}) fusion(f32[256,16,256]{2,1,0:T(8,128)} %get-tuple-element.11, f32[256,16,256]{2,1,0:T(8,128)} %get-tuple-element.5, f32[256,16,256]{2,1,0:T(8,128)} %get-tuple-element.6), kind=kLoop, calls=%fused_computation.11 | loop fusion | flops 4194304 | bytes 29360128 | tf_op jit(solution)/shard_map/concatenate | solution.py:38
  526.7 18.4 %fusion.14 = f32[16,512,256]{2,1,0:T(8,128)} fusion(f32[16,256,256]{2,1,0:T(8,128)S(1)} %copy-done.2, f32[256,16,512]{2,1,0:T(8,128)S(1)} %get-tuple-element.17), kind=kOutput, calls=%fused_computation.20 | convolution fusion | flops 6442450944 | bytes 20971520 | tf_op jit(solution)/shard_map/pay,ypz->apz/dot_general | solution.py:85
  545.1 10.5 %copy.46 = f32[16,512,256]{1,0,2:T(8,128)} copy(f32[16,512,256]{2,1,0:T(8,128)} %fusion.14) | data formatting | bytes 16777216 | tf_op jit(solution)/shard_map/pay,ypz->apz/dot_general | solution.py:85
  555.5 23.8 %fusion.16 = f32[16,512,256]{2,1,0:T(8,128)} fusion(f32[16,256,256]{2,1,0:T(8,128)} %fusion.39, f32[256,16,512]{2,1,0:T(8,128)} %get-tuple-element.18), kind=kOutput, calls=%fused_computation.22 | convolution fusion | flops 6442450944 | bytes 20971520 | tf_op jit(solution)/shard_map/pay,ypz->apz/dot_general | solution.py:82
  579.4 10.5 %copy.45 = f32[16,512,256]{1,0,2:T(8,128)} copy(f32[16,512,256]{2,1,0:T(8,128)} %fusion.16) | data formatting | bytes 16777216 | tf_op jit(solution)/shard_map/pay,ypz->apz/dot_general | solution.py:82
  589.8 9.8 %bitcast_subtract_fusion = f32[256,16,512]{2,1,0:T(8,128)S(1)} fusion(f32[256,16,512]{2,1,0:T(8,128)} %get-tuple-element.22, f32[16,512,256]{1,0,2:T(8,128)} %copy.45, f32[16,512,256]{1,0,2:T(8,128)} %copy.46), kind=kLoop, calls=%fused_computation.16 | loop fusion | flops 4194304 | bytes 33554432 | tf_op jit(solution)/shard_map/sub | solution.py:182
  599.6 4.6 multiply_add_fusion
  604.2 5.3 fusion.33
  609.5 71.4 %reduce-scatter.5.cloned.1.call-done = f32[16,8,512]{2,1,0:T(8,128)} async-done(((f32[256,8,512]{2,1,0:T(8,128)}), f32[16,8,512]{2,1,0:T(8,128)}) %reduce-scatter.5.cloned.1.call-update) | async-done | bytes 262160 | tf_op jit(solution)/shard_map/reduce_scatter | solution.py:184
  683.3 1.7 collective-permute-done.4
  685.1 2.8 collective-permute-start.5
  688.9 1.3 collective-permute-start.6
  690.2 1.7 collective-permute-done.6
  692.1 4.5 collective-permute-start.7
  (74 shorter events, 12.7 us)
Async XLA Ops:
  12.7 10.7 %copy-start.6 = (s32[8,256]{1,0:T(8,128)S(1)}, s32[8,256]{1,0:T(8,128)}, u32[]{:S(2)}) copy-start(s32[8,256]{1,0:T(8,128)} %param.7) | copy-start | bytes 24580
  12.7 183.5 %all-to-all-start = ((f32[16,256,512]{2,0,1:T(8,128)}), f32[16,256,512]{2,0,1:T(8,128)}, u32[]{:S(2)}, u32[]{:S(2)}) async-start(f32[16,256,512]{2,0,1:T(8,128)} %bitcast.60), calls=%async_computation | async-start | bytes 16777216 | tf_op jit(solution)/shard_map/all_to_all | solution.py:132
  20.3 152.1 %all-gather.3.cloned.1.call-start = ((), (), s32[]{:S(2)}) async-start(), calls=%async_computation.3 | async-start | bytes 4456448 | tf_op jit(solution)/shard_map/all_gather | solution.py:176
  21.1 410.3 %reduce-scatter.3.cloned.1.call-start = ((), (), s32[]{:S(2)}) async-start(), calls=%async_computation.4 | async-start | bytes 4456448 | tf_op jit(solution)/shard_map/reduce_scatter | solution.py:184
  32.8 14.7 %slice-start = ((s8[8388608]{0:T(1024)(128)(4,1)}), s8[4194304]{0:T(1024)(128)(4,1)S(1)}, s32[]{:S(2)}) async-start(s8[8388608]{0:T(1024)(128)(4,1)} %bitcast.61), calls=%async_computation.7 | async-start | bytes 8388608
  40.4 7.1 %slice-start.1 = ((s8[8388608]{0:T(1024)(128)(4,1)}), s8[4194304]{0:T(1024)(128)(4,1)S(1)}, s32[]{:S(2)}) async-start(s8[8388608]{0:T(1024)(128)(4,1)} %bitcast.61), calls=%async_computation.8 | async-start | bytes 8388608
  196.2 10.1 %copy-start.3 = (f32[256,16,512]{2,1,0:T(8,128)S(1)}, f32[256,16,512]{2,1,0:T(8,128)}, u32[]{:S(2)}) copy-start(f32[256,16,512]{2,1,0:T(8,128)} %convolution_bitcast_fusion.1) | copy-start | bytes 25165828
  206.3 7.1 %copy-start = (f32[16,16,16,512]{3,2,1,0:T(8,128)}, f32[16,16,16,512]{3,2,1,0:T(8,128)S(1)}, u32[]{:S(2)}) copy-start(f32[16,16,16,512]{3,2,1,0:T(8,128)S(1)} %copy.34) | copy-start | bytes 25165828
  213.4 10.3 %copy-start.1 = (f32[16,256,256]{2,1,0:T(8,128)S(1)}, f32[16,256,256]{2,1,0:T(8,128)}, u32[]{:S(2)}) copy-start(f32[16,256,256]{2,1,0:T(8,128)} %fusion.42) | copy-start | bytes 12582916
  326.6 104.8 %copy-start.5 = (f32[16,8,512]{2,1,0:T(8,128)S(1)}, f32[16,8,512]{2,1,0:T(8,128)}, u32[]{:S(2)}) copy-start(f32[16,8,512]{2,1,0:T(8,128)} %param.4) | copy-start | bytes 786436
  326.7 174.9 %all-gather.5.cloned.1.call-start = ((), (), s32[]{:S(2)}) async-start(), calls=%async_computation.5 | async-start | bytes 4456448 | tf_op jit(solution)/shard_map/all_gather | solution.py:176
  432.4 3.1 collective-permute-start
  435.6 3.5 collective-permute-start.1
  439.3 3.1 collective-permute-start.2
  442.5 5.3 collective-permute-start.3
  448.7 232.3 %reduce-scatter.5.cloned.1.call-start = ((), (), s32[]{:S(2)}) async-start(), calls=%async_computation.6 | async-start | bytes 4456448 | tf_op jit(solution)/shard_map/reduce_scatter | solution.py:184
  516.5 10.2 %copy-start.2 = (f32[16,256,256]{2,1,0:T(8,128)S(1)}, f32[16,256,256]{2,1,0:T(8,128)}, u32[]{:S(2)}) copy-start(f32[16,256,256]{2,1,0:T(8,128)} %fusion.42) | copy-start | bytes 12582916
  609.5 71.4 %copy-start.4 = (f32[16,8,512]{2,1,0:T(8,128)S(1)}, f32[16,8,512]{2,1,0:T(8,128)}, u32[]{:S(2)}) copy-start(f32[16,8,512]{2,1,0:T(8,128)} %fusion.74) | copy-start | bytes 786436
  681.9 3.1 collective-permute-start.4
  685.1 3.6 collective-permute-start.5
  688.9 3.1 collective-permute-start.6
  692.1 5.3 collective-permute-start.7
Sparse Core Ops, SparseCore 0:
  23.3 149.0 all-gather.2
  326.8 104.5 reduce-scatter.2
  448.8 52.6 all-gather.4
  609.6 71.2 reduce-scatter.4
where the time goes:
time: 717 us; the launch traced here: 705 us
  waiting for transfers between devices  351 us (49%)
  matrix products  183 us (26%)
  other arithmetic  71.3 us (10%)
  local copies, waits for them, and re-layouts  58.7 us (8%)
  starting transfers between devices  27.4 us (4%)
  between operations  14 us (2%)
    reduce_scatter x2, waiting for transfers between devices, per_device(): lax.psum_scatter(jnp.einsum('rpz,pf->rfz', weighted, onehot, precision=hi...  176 us
    all_gather x2, waiting for transfers between devices, per_device(): lax.all_gather(field, 'coil', axis=0, tiled=True)  148 us
    dot_general x2, matrix products, pair_rows(): jnp.einsum('pay,ypz->apz', proj_re, field, precision=highest, preferred_e...  47.6 us
    dot_general x2, matrix products, pair_rows(): jnp.einsum('pay,ypz->apz', proj_im, swap_parts(field), precision=highest,...  37 us
    dot_general x1, matrix products, cols_apply(): jnp.dot(flat, matrix, precision=highest, preferred_element_type=jnp.float32)  27 us
    dot_general x2, local copies, waits for them, and re-layouts, pair_rows(): jnp.einsum('pay,ypz->apz', proj_im, swap_parts(field), precision=highest,...  21 us
    dot_general x2, local copies, waits for them, and re-layouts, pair_rows(): jnp.einsum('pay,ypz->apz', proj_re, field, precision=highest, preferred_e...  20.9 us
    concatenate x2, other arithmetic, swap_parts(): return jnp.concatenate([-field[..., half:], field[..., :half]], -1)  20.5 us
  transfers between devices with their start and end apart: 13, of which 13 were waited for; matrix products, arithmetic and copies ran while one was open for 9% of the time, Pallas kernels for 0%

commit v1 on v0

v1 whole, which is shorter than its diff:
```python
import jax
import jax.numpy as jnp
from jax import lax
from jax.sharding import PartitionSpec as P

OUTER = 2
INNER = 2

step_size = 0.5
tv_weight = 0.1
dual_step = 1.25
high = lax.Precision.HIGH


def contract(spec, *operands):
    return jnp.einsum(spec, *operands, precision=high, preferred_element_type=jnp.float32)


def dft_tables(length):
    index = lax.iota(jnp.int32, length)
    product = index[:, None] * index[None, :] % length
    angle = 2.0 * jnp.pi / length * product.astype(jnp.float32)
    scale = 1.0 / jnp.sqrt(jnp.float32(length))
    return (jnp.cos(angle) * scale, -jnp.sin(angle) * scale)


def column_matrix(cos_part, sin_part):
    upper = jnp.concatenate([cos_part, sin_part], 1)
    lower = jnp.concatenate([-sin_part, cos_part], 1)
    return jnp.concatenate([upper, lower], 0)


def projections(mask, row_cos, row_sin):
    weights = mask.astype(jnp.float32)
    wide = jnp.concatenate([row_cos, row_sin], 1)
    cos_rows = weights[:, :, None] * row_cos[None]
    sin_rows = weights[:, :, None] * row_sin[None]
    from_cos = contract("fka,ky->fay", cos_rows, wide)
    from_sin = contract("fka,ky->fay", sin_rows, wide)
    length = row_cos.shape[0]
    real = from_cos[..., :length] + from_sin[..., length:]
    imag = from_cos[..., length:] - from_sin[..., :length]
    return (real, imag)


def to_columns(field, devices):
    rows, count, packed = field.shape
    width = packed // 2 // devices
    parts = field.reshape(rows, count, 2, devices, width)
    return jnp.transpose(parts, (3, 0, 2, 1, 4)).reshape(devices, rows, 2 * count * width)


def divergence(dual_time, dual_rows):
    time_axis, row_axis = 1, 3
    zero_time = jnp.zeros_like(dual_time[:, :1])
    zero_rows = jnp.zeros_like(dual_rows[..., :1])
    head_time = dual_time[:, :-1]
    head_rows = dual_rows[..., :-1]
    from_time = jnp.concatenate([zero_time, head_time], time_axis) - jnp.concatenate(
        [head_time, zero_time], time_axis
    )
    from_rows = jnp.concatenate([zero_rows, head_rows], row_axis) - jnp.concatenate(
        [head_rows, zero_rows], row_axis
    )
    return from_time + from_rows


def forward_diff(field):
    diff_time = jnp.concatenate(
        [field[:, 1:] - field[:, :-1], jnp.zeros_like(field[:, :1])], 1
    )
    diff_rows = jnp.concatenate(
        [field[..., 1:] - field[..., :-1], jnp.zeros_like(field[..., :1])], 3
    )
    return (diff_time, diff_rows)


def denoise(target):
    dual_time = jnp.zeros_like(target)
    dual_rows = jnp.zeros_like(target)
    for repeat in range(INNER):
        primal = target
        if repeat:
            primal = target - tv_weight * divergence(dual_time, dual_rows)
        diff_time, diff_rows = forward_diff(primal)
        dual_time = jnp.clip(dual_time + dual_step * diff_time, -1.0, 1.0)
        dual_rows = jnp.clip(dual_rows + dual_step * diff_rows, -1.0, 1.0)
    return target - tv_weight * divergence(dual_time, dual_rows)


def iterate(field, data_term, maps, real, imag):
    maps_re, maps_im = (maps[0][None], maps[1][None])
    for sweep in range(OUTER):
        now_re, now_im = (field[0][:, None], field[1][:, None])
        seen_re = maps_re * now_re - maps_im * now_im
        seen_im = maps_re * now_im + maps_im * now_re
        kept_re = contract("fczy,fky->fczk", seen_re, real) - contract(
            "fczy,fky->fczk", seen_im, imag
        )
        kept_im = contract("fczy,fky->fczk", seen_re, imag) + contract(
            "fczy,fky->fczk", seen_im, real
        )
        grad_re = jnp.sum(maps_re * kept_re + maps_im * kept_im, 1)
        grad_im = jnp.sum(maps_re * kept_im - maps_im * kept_re, 1)
        gradient = jnp.stack([grad_re, grad_im]) - data_term
        field = denoise(field - step_size * gradient)
    return field


def data_images(kspace, mask_pairs, row_cos, row_sin, col_cos, col_sin):
    masked = jnp.transpose(mask_pairs)[:, :, None] * kspace
    mid = contract("kpz,zw->kpw", masked, column_matrix(col_cos, -col_sin))
    half = kspace.shape[-1] // 2
    from_cos = contract("ky,kpz->ypz", row_cos, mid)
    from_sin = contract("ky,kpz->ypz", row_sin, mid)
    real = from_cos[..., :half] + from_sin[..., half:]
    imag = from_cos[..., half:] - from_sin[..., :half]
    return (real, imag)


def per_device(image, sens, kspace, mask):
    devices = lax.axis_size("coil")
    device = lax.axis_index("coil")
    rows_dev, frames, packed = image.shape
    coils = sens.shape[1]
    length, pairs, unused = kspace.shape
    half = packed // 2
    width = half // devices
    copies = max(1, frames // pairs)
    own_coils = max(1, pairs // frames)
    own_frames = min(frames, pairs)
    row_cos, row_sin = dft_tables(length)
    col_cos, col_sin = dft_tables(half)

    spread = sens if copies == 1 else jnp.repeat(sens, copies, axis=1)
    own_maps = lax.all_to_all(spread, "coil", split_axis=1, concat_axis=0, tiled=True)
    outgoing = jnp.concatenate([to_columns(sens, devices), to_columns(image, devices)], 2)
    incoming = lax.all_to_all(outgoing, "coil", split_axis=0, concat_axis=0, tiled=True)
    columns = jnp.transpose(incoming.reshape(length, -1))
    cut = 2 * coils * width
    maps = columns[:cut].reshape(2, coils, width, length)
    field = columns[cut:].reshape(2, frames, width, length)

    first_frame = device * pairs % frames
    mask_float = mask.astype(jnp.float32)
    local_mask = lax.dynamic_slice_in_dim(mask_float, first_frame, own_frames, 0)
    mask_pairs = jnp.tile(local_mask, (own_coils, 1))
    base_re, base_im = data_images(kspace, mask_pairs, row_cos, row_sin, col_cos, col_sin)
    base_re = base_re.reshape(length, own_coils, own_frames, half)
    base_im = base_im.reshape(length, own_coils, own_frames, half)
    own_re, own_im = (own_maps[:, :, None, :half], own_maps[:, :, None, half:])
    term_re = jnp.sum(own_re * base_re + own_im * base_im, 1)
    term_im = jnp.sum(own_re * base_im - own_im * base_re, 1)
    term = jnp.transpose(jnp.stack([term_re, term_im]), (3, 0, 2, 1))
    if own_frames < frames:
        wide = jnp.zeros((half, 2, frames, length), jnp.float32)
        term = lax.dynamic_update_slice_in_dim(wide, term, first_frame, 2)
    term = term.reshape(devices, width, 2, frames, length)
    data_term = lax.psum_scatter(term, "coil", scatter_dimension=0, tiled=True)
    data_term = jnp.transpose(data_term[0], (1, 2, 0, 3))

    real, imag = projections(mask, row_cos, row_sin)
    field = iterate(field, data_term, maps, real, imag)

    leaving = jnp.transpose(field.reshape(2 * frames * width, length))
    leaving = leaving.reshape(devices, rows_dev, 2 * frames * width)
    arrived = lax.all_to_all(leaving, "coil", split_axis=0, concat_axis=0, tiled=True)
    arrived = arrived.reshape(devices, rows_dev, 2, frames, width)
    return jnp.transpose(arrived, (1, 3, 2, 0, 4)).reshape(rows_dev, frames, packed)


def solution(mesh):
    return jax.shard_map(
        per_device,
        mesh=mesh,
        in_specs=(
            P(("plane", "coil"), None, None),
            P(("plane", "coil"), None, None),
            P("plane", "coil", None),
            P(),
        ),
        out_specs=P(("plane", "coil"), None, None),
        check_vma=False,
    )
```

time: 717 us -> 230 us (0.32); the launches traced: 705 us -> 226 us
  waiting for transfers between devices: 351 us -> 35.9 us
  matrix products: 183 us -> 57.9 us
  other arithmetic: 71.3 us -> 28.8 us
  blocking collectives: 0 us -> 17.6 us
  starting transfers between devices: 27.4 us -> 13.7 us
    reduce_scatter x2 -> x1, waiting for transfers between devices: 176 us -> 0.01 us  [per_device(): data_term = lax.psum_scatter(term, 'coil', scatter_dimension=0, tiled=True)]
    all_gather x2 -> x0, waiting for transfers between devices: 148 us -> none  [per_device(): lax.all_gather(field, 'coil', axis=0, tiled=True)]
    dot_general x16 -> x13, matrix products: 183 us -> 57.9 us  [contract(): jnp.einsum(spec, *operands, precision=high, preferred_element_type=jnp.fl...]
    dot_general x4 -> x0, local copies, waits for them, and re-layouts: 41.9 us -> none  [the longest x2 21 us: pair_rows(): jnp.einsum('pay,ypz->apz', proj_im, swap_parts(field), precision=highest,...]
    reshape x0 -> x7, local copies, waits for them, and re-layouts: none -> 25.7 us  [the longest x2 8.99 us: to_columns(): jnp.transpose(parts, (3, 0, 2, 1, 4))]
    all_to_all x1 -> x2, waiting for transfers between devices: 16.2 us -> 35.8 us  [the longest x1 35.8 us: per_device(): lax.all_to_all(outgoing, 'coil', split_axis=0, concat_axis=0, tiled=True)]
    ppermute x8 -> x0, starting transfers between devices: 19.6 us -> none  [shifted(): return lax.ppermute(block, axis, route)]
    concatenate x2 -> x1, other arithmetic: 20.5 us -> 1.18 us  [per_device(): jnp.concatenate([to_columns(sens, devices), to_columns(image, devices)], 2)]
  transfers between devices with their start and end apart: 13 -> 3, of which waited for: 13 -> 1; matrix products, arithmetic and copies ran while one was open for 9% -> 43% of each run, Pallas kernels for 0% -> 0%
where the time goes in v1:
time: 230 us; the launch traced here: 226 us
  local copies, waits for them, and re-layouts  58.1 us (25%)
  matrix products  57.9 us (25%)
  waiting for transfers between devices  35.9 us (16%)
  other arithmetic  28.8 us (13%)
  blocking collectives  17.6 us (8%)
  between operations  14.2 us (6%)
  starting transfers between devices  13.7 us (6%)
    dot_general x13, matrix products, contract(): jnp.einsum(spec, *operands, precision=high, preferred_element_type=jnp.fl...  57.9 us
    all_to_all x1, waiting for transfers between devices, per_device(): lax.all_to_all(outgoing, 'coil', split_axis=0, concat_axis=0, tiled=True)  35.8 us
    all_to_all x1, blocking collectives, per_device(): lax.all_to_all(leaving, 'coil', split_axis=0, concat_axis=0, tiled=True)  17.6 us
    add x1, other arithmetic, data_images(): real = from_cos[..., :half] + from_sin[..., half:]  10.5 us
    unnamed x20, local copies, waits for them, and re-layouts  9.55 us
    reshape x2, local copies, waits for them, and re-layouts, to_columns(): jnp.transpose(parts, (3, 0, 2, 1, 4))  8.99 us
    all_to_all x1, starting transfers between devices, per_device(): lax.all_to_all(spread, 'coil', split_axis=1, concat_axis=0, tiled=True)  7.41 us
    reshape x1, local copies, waits for them, and re-layouts, per_device(): term = term.reshape(devices, width, 2, frames, length)  7.4 us
  transfers between devices with their start and end apart: 3, of which 1 were waited for; matrix products, arithmetic and copies ran while one was open for 43% of the time, Pallas kernels for 0%

profile of v1, /device:TPU:0, one launch (start us, length us, event | category | flops | bytes accessed | tf_op | source)
XLA Modules:
  0.0 226.2 jit_solution(4659679379708129776)
XLA Ops:
  6.5 2.9 %copy.56 = f32[16,32,512]{2,0,1:T(8,128)} copy(f32[16,32,512]{2,1,0:T(8,128)} %param.5) | data formatting | bytes 2097152 | tf_op args[1]
  9.4 7.4 %all-to-all-start.1 = ((f32[16,32,512]{2,0,1:T(8,128)}), f32[16,32,512]{2,0,1:T(8,128)S(1)}, u32[]{:S(2)}, u32[]{:S(2)}) async-start(f32[16,32,512]{2,0,1:T(8,128)} %copy.56), calls=%async_computation.1 | async-start | bytes 2097152 | tf_op jit(solution)/shard_map/all_to_all | solution.py:136
  16.9 1.1 negate_multiply_fusion
  18.0 1.0 fusion.76
  19.1 4.0 %broadcast_multiply_fusion = f32[256,16,512]{2,1,0:T(8,128)S(1)} fusion(f32[256,16,512]{2,1,0:T(8,128)} %param.6, f32[256,16]{1,0:T(8,128)S(1)} %copy.58), kind=kLoop, calls=%fused_computation.15 | loop fusion | flops 2097152 | bytes 16793600 | tf_op jit(solution)/shard_map/mul | solution.py:111
  23.1 10.7 %fusion = f32[256,16,512]{2,0,1:T(8,128)S(1)} fusion(f32[256,16,512]{2,1,0:T(8,128)S(1)} %broadcast_multiply_fusion, f32[256,256]{1,0:T(8,128)S(1)} %get-tuple-element.24, f32[256,256]{1,0:T(8,128)S(1)} %get-tuple-element.23, f32[256,256]{1,0:T(8,128)S(1)} %fusion.76), kind=kOutput, calls=%fused_computation | convolution fusion | flops 6443237376 | bytes 17563648 | tf_op jit(solution)/shard_map/kpz,zw->kpw/dot_general | solution.py:16
  33.8 8.7 %fusion.69 = f32[256,16,512]{2,0,1:T(8,128)} fusion(f32[256,16,512]{2,0,1:T(8,128)S(1)} %fusion), kind=kOutput, calls=%fused_computation.98 | convolution fusion | flops 3222274048 | bytes 16777216 | tf_op jit(solution)/shard_map/ky,kpz->ypz/dot_general | solution.py:16
  42.5 8.4 %fusion.71 = f32[256,16,512]{2,0,1:T(8,128)} fusion(f32[256,16,512]{2,0,1:T(8,128)S(1)} %fusion), kind=kOutput, calls=%fused_computation.100 | convolution fusion | flops 3222208512 | bytes 16777216 | tf_op jit(solution)/shard_map/ky,kpz->ypz/dot_general | solution.py:16
  50.9 10.5 %slice_add_fusion = (f32[256,16,256]{2,0,1:T(8,128)}, f32[256,16,256]{2,0,1:T(8,128)}) fusion(f32[256,16,512]{2,0,1:T(8,128)} %fusion.69, f32[256,16,512]{2,0,1:T(8,128)} %fusion.71), kind=kLoop, calls=%fused_computation.3 | loop fusion | flops 2097152 | bytes 25165824 | tf_op jit(solution)/shard_map/add | solution.py:116
  61.7 2.0 copy-done.2
  63.7 4.0 %add_reduce_fusion.1 = (f32[256,8,256]{2,0,1:T(8,128)S(1)}, f32[256,8,256]{2,0,1:T(8,128)S(1)}) fusion(f32[256,2,8,256]{3,0,2,1:T(8,128)} %bitcast.107, f32[256,2,8,256]{3,0,2,1:T(8,128)S(1)} %bitcast.106, f32[256,2,256]{2,0,1:T(8,128)S(1)} %get-tuple-element.20, f32[256,2,256]{2,0,1:T(8,128)S(1)} %get-tuple-element.19), kind=kLoop, calls=%fused_computation.14 | loop fusion | flops 7340032 | bytes 13631488 | tf_op jit(solution)/shard_map/reduce_sum | solution.py:152
  67.7 2.3 %maximum_bitcast_fusion = f32[256,2,8,256]{0,3,2,1:T(8,128)} fusion(f32[1,256,8,256]{3,1,2,0:T(8,128)S(1)} %bitcast.111, f32[1,256,8,256]{3,1,2,0:T(8,128)S(1)} %bitcast.110), kind=kLoop, calls=%fused_computation.4 | loop fusion | flops 1048576 | bytes 8388608 | tf_op jit(solution)/shard_map/transpose | solution.py:154
  70.0 5.9 %copy.62 = f32[256,2,8,256]{3,2,1,0:T(8,128)} copy(f32[256,2,8,256]{0,3,2,1:T(8,128)} %maximum_bitcast_fusion) | data formatting | bytes 8388608 | tf_op jit(solution)/shard_map/transpose | solution.py:154
  75.8 7.4 %copy.63 = f32[16,16,2,8,256]{4,1,3,2,0:T(8,128)} copy(f32[16,16,2,8,256]{4,3,2,1,0:T(8,128)} %bitcast.105) | data formatting | bytes 8388608 | tf_op jit(solution)/shard_map/reshape | solution.py:158
  83.3 1.2 copy-done.3
  84.5 2.6 %copy.46 = f32[16,32,512]{1,2,0:T(8,128)} copy(f32[16,32,512]{2,1,0:T(8,128)S(1)} %copy-done.3) | data formatting | bytes 2097152 | tf_op args[1]
  87.1 2.1 reshape.101
  89.2 3.0 %copy.75 = f32[16,8,2,16,16]{4,1,2,0,3:T(8,128)S(1)} copy(f32[16,8,2,16,16]{4,3,2,1,0:T(8,128)} %reshape.101) | data formatting | bytes 524288 | tf_op jit(solution)/shard_map/reshape | solution.py:49
  92.1 0.9 reshape.102
  93.1 7.1 %copy.47 = f32[16,16,2,32,16]{4,3,2,1,0:T(8,128)} copy(f32[16,16,2,32,16]{3,4,0,2,1:T(8,128)} %bitcast.104) | data formatting | bytes 2097152 | tf_op jit(solution)/shard_map/transpose | solution.py:50
  100.2 8.1 %reshape.100 = f32[16,16,1024]{2,1,0:T(8,128)S(1)} reshape(f32[16,16,2,32,16]{4,3,2,1,0:T(8,128)} %copy.47) | data formatting | bytes 2097152 | tf_op jit(solution)/shard_map/reshape | solution.py:50
  108.3 1.2 pad_maximum_fusion
  109.5 6.2 %all-to-all-start = ((f32[16,16,1280]{2,1,0:T(8,128)}), f32[16,16,1280]{2,1,0:T(8,128)}, u32[]{:S(2)}, u32[]{:S(2)}) async-start(f32[16,16,1280]{2,1,0:T(8,128)} %pad_maximum_fusion), calls=%async_computation | async-start | bytes 2621440 | tf_op jit(solution)/shard_map/all_to_all | solution.py:138
  116.0 1.9 fusion.22
  117.9 1.9 fusion.24
  119.9 2.0 fusion.10
  121.8 35.8 %all-to-all-done = f32[16,16,1280]{2,1,0:T(8,128)} async-done(((f32[16,16,1280]{2,1,0:T(8,128)}), f32[16,16,1280]{2,1,0:T(8,128)}, u32[]{:S(2)}, u32[]{:S(2)}) %all-to-all-start) | async-done | bytes 1310752 | tf_op jit(solution)/shard_map/all_to_all | solution.py:138
  157.7 1.0 slice.181
  158.6 0.8 copy.49
  159.5 1.0 fusion.91
  160.6 2.1 fusion.90
  162.6 0.2 copy.52
  163.0 1.2 copy.50
  164.2 4.0 %fusion.7 = f32[8,32,16,256]{3,2,1,0:T(8,128)S(1)} fusion(f32[8,256,256,1]{2,1,3,0:T(8,128)} %get-tuple-element.13, f32[8,16,256]{2,1,0:T(8,128)S(1)} %bitcast.116, f32[32,16,256]{2,1,0:T(8,128)S(1)} %bitcast.88, f32[8,16,256]{2,1,0:T(8,128)S(1)} %bitcast.120, f32[32,16,256]{2,1,0:T(8,128)S(1)} %bitcast.96), kind=kOutput, calls=%fused_computation.20 | convolution fusion | flops 1613758464 | bytes 7602176 | tf_op jit(solution)/shard_map/fczy,fky->fczk/dot_general | solution.py:16
  168.3 2.4 %fusion.6 = f32[8,32,16,256]{3,2,1,0:T(8,128)S(1)} fusion(f32[8,256,256,1]{2,1,3,0:T(8,128)S(1)} %get-tuple-element.14, f32[8,16,256]{2,1,0:T(8,128)S(1)} %bitcast.117, f32[32,16,256]{2,1,0:T(8,128)S(1)} %bitcast.89, f32[8,16,256]{2,1,0:T(8,128)S(1)} %bitcast.121, f32[32,16,256]{2,1,0:T(8,128)S(1)} %bitcast.97), kind=kOutput, calls=%fused_computation.19 | convolution fusion | flops 1613758464 | bytes 7602176 | tf_op jit(solution)/shard_map/fczy,fky->fczk/dot_general | solution.py:16
  170.7 2.8 %fusion.30 = f32[8,32,16,256]{3,2,1,0:T(8,128)S(1)} fusion(f32[8,32,16,256]{3,2,1,0:T(8,128)S(1)} %fusion.7, f32[8,256,256,1]{2,1,3,0:T(8,128)S(1)} %get-tuple-element.14, f32[8,16,256]{2,1,0:T(8,128)S(1)} %bitcast.118, f32[32,16,256]{2,1,0:T(8,128)S(1)} %bitcast.90, f32[8,16,256]{2,1,0:T(8,128)S(1)} %bitcast.122, f32[32,16,256]{2,1,0:T(8,128)S(1)} %bitcast.98), kind=kOutput, calls=%fused_computation.47 | convolution fusion | flops 1614807040 | bytes 11796480 | tf_op jit(solution)/shard_map/fczy,fky->fczk/dot_general | solution.py:16
  173.5 4.9 %add_reduce_fusion.2 = (f32[8,16,256]{2,1,0:T(8,128)S(1)}, f32[8,16,256]{2,1,0:T(8,128)}) fusion(f32[8,32,16,256]{3,2,1,0:T(8,128)S(1)} %fusion.30, f32[32,16,256]{2,1,0:T(8,128)S(1)} %bitcast.91, f32[32,16,256]{2,1,0:T(8,128)S(1)} %bitcast.99, f32[8,32,16,256]{3,2,1,0:T(8,128)S(1)} %fusion.6, f32[8,256,256,1]{2,1,3,0:T(8,128)S(1)} %copy-done, ...), kind=kOutput, calls=%fused_computation.17 | convolution fusion | flops 1623130112 | bytes 12058624 | tf_op jit(solution)/shard_map/fczy,fky->fczk/dot_general | solution.py:16
  178.4 1.2 fusion.66
  179.9 0.2 multiply_subtract_fusion.17
  180.5 0.8 copy-done.1
  181.3 2.5 %fusion.3 = f32[8,32,16,256]{3,2,1,0:T(8,128)S(1)} fusion(f32[8,256,256,1]{2,1,3,0:T(8,128)S(1)} %copy-done.1, f32[8,16,256]{2,1,0:T(8,128)S(1)} %get-tuple-element.22, f32[8,16,256]{2,1,0:T(8,128)S(1)} %get-tuple-element.21, f32[32,16,256]{2,1,0:T(8,128)S(1)} %bitcast.92, f32[32,16,256]{2,1,0:T(8,128)S(1)} %bitcast.100), kind=kOutput, calls=%fused_computation.9 | convolution fusion | flops 1613758464 | bytes 7602176 | tf_op jit(solution)/shard_map/fczy,fky->fczk/dot_general | solution.py:16
  183.9 2.5 %fusion.2 = f32[8,32,16,256]{3,2,1,0:T(8,128)S(1)} fusion(f32[8,256,256,1]{2,1,3,0:T(8,128)S(1)} %get-tuple-element.14, f32[8,16,256]{2,1,0:T(8,128)S(1)} %get-tuple-element.22, f32[8,16,256]{2,1,0:T(8,128)S(1)} %get-tuple-element.21, f32[32,16,256]{2,1,0:T(8,128)S(1)} %bitcast.93, f32[32,16,256]{2,1,0:T(8,128)S(1)} %bitcast.101), kind=kOutput, calls=%fused_computation.8 | convolution fusion | flops 1613758464 | bytes 7602176 | tf_op jit(solution)/shard_map/fczy,fky->fczk/dot_general | solution.py:16
  186.3 2.6 %fusion.16 = f32[8,32,16,256]{3,2,1,0:T(8,128)S(1)} fusion(f32[8,32,16,256]{3,2,1,0:T(8,128)S(1)} %fusion.3, f32[8,256,256,1]{2,1,3,0:T(8,128)S(1)} %get-tuple-element.14, f32[8,16,256]{2,1,0:T(8,128)S(1)} %get-tuple-element.22, f32[8,16,256]{2,1,0:T(8,128)S(1)} %get-tuple-element.21, f32[32,16,256]{2,1,0:T(8,128)S(1)} %bitcast.94, ...), kind=kOutput, calls=%fused_computation.33 | convolution fusion | flops 1614807040 | bytes 11796480 | tf_op jit(solution)/shard_map/fczy,fky->fczk/dot_general | solution.py:16
  189.0 4.5 %add_reduce_fusion = (f32[8,16,256]{2,1,0:T(8,128)S(1)}, f32[8,16,256]{2,1,0:T(8,128)S(1)}) fusion(f32[8,32,16,256]{3,2,1,0:T(8,128)S(1)} %fusion.16, f32[32,16,256]{2,1,0:T(8,128)S(1)} %bitcast.95, f32[32,16,256]{2,1,0:T(8,128)S(1)} %bitcast.103, f32[8,32,16,256]{3,2,1,0:T(8,128)S(1)} %fusion.2, f32[8,256,256,1]{2,1,3,0:T(8,128)S(1)} %copy-done.1, ...), kind=kOutput, calls=%fused_computation.6 | convolution fusion | flops 1623130112 | bytes 12058624 | tf_op jit(solution)/shard_map/fczy,fky->fczk/dot_general | solution.py:16
  194.6 17.6 %all_to_all.28 = f32[16,16,256]{2,1,0:T(8,128)S(1)} all-to-all(f32[16,16,256]{2,1,0:T(8,128)S(1)} %bitcast.126), channel_id=1, replica_groups=mesh['plane'=2,'coil'=16] {'coil'}, dimensions={0} | all-to-all | bytes 524288 | tf_op jit(solution)/shard_map/all_to_all | solution.py:167
  212.2 0.6 reshape.110
  212.8 2.6 %copy.65 = f32[16,8,2,16,16]{4,3,2,1,0:T(8,128)} copy(f32[16,8,2,16,16]{4,1,2,0,3:T(8,128)S(1)} %bitcast.109) | data formatting | bytes 524288 | tf_op jit(solution)/shard_map/transpose | solution.py:169
  215.4 3.7 %reshape.111 = f32[16,8,512]{2,1,0:T(8,128)} reshape(f32[16,8,2,16,16]{4,3,2,1,0:T(8,128)} %copy.65) | data formatting | bytes 524288 | tf_op jit(solution)/shard_map/reshape | solution.py:169
  (54 shorter events, 2.5 us)
Async XLA Ops:
  6.5 12.4 %copy-start.8 = (s32[8,256]{1,0:T(8,128)S(1)}, s32[8,256]{1,0:T(8,128)}, u32[]{:S(2)}) copy-start(s32[8,256]{1,0:T(8,128)} %param.7) | copy-start | bytes 24580
  9.4 52.0 %all-to-all-start.1 = ((f32[16,32,512]{2,0,1:T(8,128)}), f32[16,32,512]{2,0,1:T(8,128)S(1)}, u32[]{:S(2)}, u32[]{:S(2)}) async-start(f32[16,32,512]{2,0,1:T(8,128)} %copy.56), calls=%async_computation.1 | async-start | bytes 2097152 | tf_op jit(solution)/shard_map/all_to_all | solution.py:136
  16.8 161.6 %reduce-scatter.2.cloned.1.call-start = ((), (), s32[]{:S(2)}) async-start(), calls=%async_computation.4 | async-start | bytes 4456448 | tf_op jit(solution)/shard_map/reduce_scatter | solution.py:159
  61.5 2.2 copy-start.2
  83.2 1.2 copy-start.3
  83.2 3.9 %copy-start.5 = (f32[16,8,512]{2,1,0:T(8,128)S(1)}, f32[16,8,512]{2,1,0:T(8,128)}, u32[]{:S(2)}) copy-start(f32[16,8,512]{2,1,0:T(8,128)} %param.4) | copy-start | bytes 786436
  109.5 48.2 %all-to-all-start = ((f32[16,16,1280]{2,1,0:T(8,128)}), f32[16,16,1280]{2,1,0:T(8,128)}, u32[]{:S(2)}, u32[]{:S(2)}) async-start(f32[16,16,1280]{2,1,0:T(8,128)} %pad_maximum_fusion), calls=%async_computation | async-start | bytes 2621440 | tf_op jit(solution)/shard_map/all_to_all | solution.py:138
  170.7 2.8 %copy-start = (f32[8,256,256,1]{2,1,3,0:T(8,128)S(1)}, f32[8,256,256,1]{2,1,3,0:T(8,128)}, u32[]{:S(2)}) copy-start(f32[8,256,256,1]{2,1,3,0:T(8,128)} %get-tuple-element.13) | copy-start | bytes 6291460
  173.5 6.3 %copy-start.6 = (pred[8]{0:T(512)(128)(4,1)S(1)}, pred[8]{0:T(512)(128)(4,1)}, u32[]{:S(2)}) copy-start(pred[8]{0:T(512)(128)(4,1)} %constant.56.clone.1) | copy-start | bytes 28
  173.5 6.3 %copy-start.7 = (pred[256]{0:T(512)(128)(4,1)S(1)}, pred[256]{0:T(512)(128)(4,1)}, u32[]{:S(2)}) copy-start(pred[256]{0:T(512)(128)(4,1)} %constant.57.clone.1) | copy-start | bytes 772
  179.7 1.6 copy-start.1
  189.0 4.5 %copy-start.4 = (f32[1,16,2,8,256]{4,1,3,2,0:T(8,128)S(1)}, f32[1,16,2,8,256]{4,1,3,2,0:T(8,128)}, u32[]{:S(2)}) copy-start(f32[1,16,2,8,256]{4,1,3,2,0:T(8,128)} %reduce-scatter.2.cloned.1.call-done) | copy-start | bytes 786436
Sparse Core Ops, SparseCore 0:
  83.4 92.2 reduce-scatter.1
